TPU v7x, 32 devices: a whole 2x2x4 slice. The times are simulated.
32 devices in a mesh: lang: 8 (over z, core), batch: 4 (over y, x).
Axes of the slice: x: 2, y: 2, z: 4, core: 2. Of those that a mesh axis runs over, the one named last changes fastest.
Arguments:
- dec_states: bfloat16 [8, 48, 32, 1024], P('lang', 'batch'), may hold values from -6 to 6
- grad_out: bfloat16 [8, 48, 32, 1024], P('lang', 'batch'), may hold values from -6 to 6
- enc_rows: bfloat16 [8, 24, 128, 1024], P('lang', 'batch'), may hold values from -6 to 6
- source_lengths: int32 [8, 24], P('lang', 'batch'), may hold values from 1 to 128, as said below
- pair_counts: int32 [8, 8], replicated, may hold values from 0 to 2, as said below
- query_gain: float32 [8, 1024], P('lang'), may hold values from 0.5 to 1.5
- w_query: bfloat16 [8, 1024, 512], P('lang', 'batch'), may hold values from -0.1875 to 0.1875
- w_key: bfloat16 [8, 1024, 512], P('lang', 'batch'), may hold values from -0.1875 to 0.1875
- w_value: bfloat16 [8, 1024, 512], P('lang', 'batch'), may hold values from -0.1875 to 0.1875
- w_out: bfloat16 [8, 512, 1024], P('lang', 'batch'), may hold values from -0.25 to 0.25
Outputs:
- attended: bfloat16 [8, 48, 32, 1024], P('lang', 'batch')
- dec_grad: bfloat16 [8, 48, 32, 1024], P('lang', 'batch')
- enc_grad: bfloat16 [8, 24, 128, 1024], P('lang', 'batch')
- gain_grad: float32 [8, 1024], P('lang', 'batch')
- query_grad: float32 [8, 1024, 512], P('lang', 'batch')
- key_grad: float32 [8, 1024, 512], P('lang', 'batch')
- value_grad: float32 [8, 1024, 512], P('lang', 'batch')
- out_grad: float32 [8, 512, 1024], P('lang', 'batch')
Inputs may be any that keep to these rules, and one draw needn't show every extreme that they name: `pair_counts`: each row sums to 6; a device's sentences are ordered by target language; no column sums to more than 12 and some column sums to exactly 12; no entry exceeds 2, and some entry equals it. `source_lengths`: on every device some sentence has 128 real tokens and some has 1.
All inputs are finite; a program needn't handle non-finite values.
Results may differ from a plain program's by a relative error of at most 0.02.
Values may be sent and summed in bfloat16 or wider, within the bound.
No kernel may reach another device: no remote copies, remote signals or barrier semaphores. Data moves between devices by JAX's collectives and lax.ppermute only.
A program may use at most 128 MiB of HBM per device.

v0:
```python
import jax
import jax.numpy as jnp
from jax import lax
from jax.sharding import PartitionSpec as P

HEADS = 8
HDIM = 64


def cross_branch(states, query_gain, w_query, w_key, w_value, w_out, memory, key_lengths):
    slot_count = states.shape[0]
    states32 = states.astype(jnp.float32)
    scale_inv = lax.rsqrt(jnp.mean(states32 * states32, axis=-1, keepdims=True) + 1e-06)
    normed = (states32 * scale_inv * query_gain).astype(jnp.bfloat16)
    queries = jnp.einsum("ktd,de->kte", normed, w_query, preferred_element_type=jnp.float32).astype(
        jnp.bfloat16
    )
    key_rows = jnp.einsum("ksd,de->kse", memory, w_key, preferred_element_type=jnp.float32).astype(
        jnp.bfloat16
    )
    value_rows = jnp.einsum(
        "ksd,de->kse", memory, w_value, preferred_element_type=jnp.float32
    ).astype(jnp.bfloat16)
    queries = queries.reshape(slot_count, queries.shape[1], HEADS, HDIM)
    key_rows = key_rows.reshape(slot_count, key_rows.shape[1], HEADS, HDIM)
    value_rows = value_rows.reshape(slot_count, value_rows.shape[1], HEADS, HDIM)
    scores = jnp.einsum(
        "kthe,kshe->khts", queries, key_rows, preferred_element_type=jnp.float32
    ) * HDIM ** (-0.5)
    key_live = jnp.arange(key_rows.shape[1], dtype=jnp.int32)[None, :] < key_lengths[:, None]
    raised = jnp.where(key_live[:, None, None, :], jnp.exp(scores), 0.0)
    empty_slot = (key_lengths == 0).astype(jnp.float32)[:, None, None, None]
    shares = (raised / (jnp.sum(raised, axis=-1, keepdims=True) + empty_slot)).astype(jnp.bfloat16)
    context = jnp.einsum(
        "khts,kshe->kthe", shares, value_rows, preferred_element_type=jnp.float32
    ).astype(jnp.bfloat16)
    context = context.reshape(slot_count, context.shape[1], HEADS * HDIM)
    return jnp.einsum("kte,ed->ktd", context, w_out, preferred_element_type=jnp.float32)


def device_step(states, upstream, query_gain, w_query, w_key, w_value, w_out, memory, key_lengths):

    def branch_fn(states_in, gain_in, query_in, key_in, value_in, out_in, memory_in):
        return cross_branch(
            states_in, gain_in, query_in, key_in, value_in, out_in, memory_in, key_lengths
        )

    branch, backward = jax.vjp(
        branch_fn, states, query_gain, w_query, w_key, w_value, w_out, memory
    )
    gradients = backward(upstream.astype(jnp.float32))
    state_grad = (upstream.astype(jnp.float32) + gradients[0].astype(jnp.float32)).astype(
        jnp.bfloat16
    )
    return (branch.astype(jnp.bfloat16), state_grad, gradients[1:])


def per_device(
    dec_states,
    grad_out,
    enc_rows,
    source_lengths,
    pair_counts,
    query_gain,
    w_query,
    w_key,
    w_value,
    w_out,
):
    lang_count = lax.axis_size("lang")
    lang_index = lax.axis_index("lang")
    sent_count = enc_rows.shape[1]
    live_cap = dec_states.shape[1]
    pair_cap = (live_cap + lang_count - 1) // lang_count
    seq_len = enc_rows.shape[2]
    model_width = enc_rows.shape[3]
    full_query, full_key, full_value, full_out = (
        lax.all_gather(w_query, "batch", axis=1, tiled=True),
        lax.all_gather(w_key, "batch", axis=1, tiled=True),
        lax.all_gather(w_value, "batch", axis=1, tiled=True),
        lax.all_gather(w_out, "batch", axis=1, tiled=True),
    )
    send_counts = lax.dynamic_index_in_dim(pair_counts, lang_index, 0, keepdims=False)
    send_start = jnp.cumsum(send_counts) - send_counts
    pair_slots = jnp.arange(pair_cap, dtype=jnp.int32)[None, :]
    sending = pair_slots < send_counts[:, None]
    picked = jnp.clip(send_start[:, None] + pair_slots, 0, sent_count - 1)
    send_rows = jnp.where(
        sending[:, :, None, None], enc_rows[0][picked], jnp.zeros((), jnp.bfloat16)
    )
    send_lengths = jnp.where(sending, source_lengths[0][picked], 0).astype(jnp.bfloat16)
    got_rows, got_lengths = (
        lax.all_to_all(send_rows, "lang", split_axis=0, concat_axis=0, tiled=True),
        lax.all_to_all(send_lengths, "lang", split_axis=0, concat_axis=0, tiled=True),
    )
    recv_counts = lax.dynamic_index_in_dim(pair_counts, lang_index, 1, keepdims=False)
    recv_start = jnp.cumsum(recv_counts) - recv_counts
    slot_ids = jnp.arange(live_cap, dtype=jnp.int32)
    source_of = jnp.sum(
        (jnp.cumsum(recv_counts)[None, :] <= slot_ids[:, None]).astype(jnp.int32), axis=1
    )
    source_of = jnp.minimum(source_of, lang_count - 1)
    is_valid = slot_ids < jnp.sum(recv_counts)
    flat_slot = jnp.clip(
        source_of * pair_cap + slot_ids - recv_start[source_of], 0, lang_count * pair_cap - 1
    )
    got_flat = got_rows.reshape(lang_count * pair_cap, seq_len, model_width)
    memory = jnp.where(is_valid[:, None, None], got_flat[flat_slot], jnp.zeros((), jnp.bfloat16))
    key_lengths = jnp.where(
        is_valid, got_lengths.reshape(-1)[flat_slot].astype(jnp.float32), 0.0
    ).astype(jnp.int32)
    branch, state_grad, gradients = device_step(
        dec_states[0],
        grad_out[0],
        query_gain[0],
        full_query[0],
        full_key[0],
        full_value[0],
        full_out[0],
        memory,
        key_lengths,
    )
    gain_part, query_part, key_part, value_part, out_part, memory_grad = gradients
    back_slot = jnp.clip(recv_start[:, None] + pair_slots, 0, live_cap - 1)
    returning = pair_slots < recv_counts[:, None]
    back_rows = jnp.where(
        returning[:, :, None, None], memory_grad[back_slot], jnp.zeros((), jnp.bfloat16)
    )
    came_back = lax.all_to_all(back_rows, "lang", split_axis=0, concat_axis=0, tiled=True)
    sentence_ids = jnp.arange(sent_count, dtype=jnp.int32)
    target_of = jnp.sum(
        (jnp.cumsum(send_counts)[None, :] <= sentence_ids[:, None]).astype(jnp.int32), axis=1
    )
    back_index = target_of * pair_cap + sentence_ids - send_start[target_of]
    enc_grad = came_back.reshape(lang_count * pair_cap, seq_len, model_width)[back_index]
    summed = (
        lax.psum(query_part, "batch").astype(jnp.float32),
        lax.psum(key_part, "batch").astype(jnp.float32),
        lax.psum(value_part, "batch").astype(jnp.float32),
        lax.psum(out_part, "batch").astype(jnp.float32),
        lax.psum(gain_part.astype(jnp.bfloat16), "batch").astype(jnp.float32),
    )
    batch_count = lax.axis_size("batch")
    batch_index = lax.axis_index("batch")
    totals = tuple(
        (
            lax.dynamic_slice_in_dim(
                whole_sum,
                batch_index * (whole_sum.shape[0] // batch_count),
                whole_sum.shape[0] // batch_count,
                0,
            )
            for whole_sum in summed
        )
    )
    return (
        branch[None],
        state_grad[None],
        enc_grad[None],
        totals[4][None],
        totals[0][None],
        totals[1][None],
        totals[2][None],
        totals[3][None],
    )


def solution(mesh):
    return jax.shard_map(
        per_device,
        mesh=mesh,
        in_specs=(
            P("lang", "batch", None, None),
            P("lang", "batch", None, None),
            P("lang", "batch", None, None),
            P("lang", "batch"),
            P(),
            P("lang", None),
            P("lang", "batch", None),
            P("lang", "batch", None),
            P("lang", "batch", None),
            P("lang", "batch", None),
        ),
        out_specs=(
            P("lang", "batch", None, None),
            P("lang", "batch", None, None),
            P("lang", "batch", None, None),
            P("lang", "batch"),
            P("lang", "batch", None),
            P("lang", "batch", None),
            P("lang", "batch", None),
            P("lang", "batch", None),
        ),
        check_vma=False,
    )
```

profile of v0, /device:TPU:0, one launch (start us, length us, event | category | flops | bytes accessed | tf_op | source)
XLA Modules:
  0.0 305.7 jit_solution(16203825089451757280)
XLA Ops:
  11.2 6.4 %all-to-all-start.1 = ((bf16[8,1,2]{2,1,0:T(2,128)(2,1)}), bf16[8,1,2]{2,1,0:T(2,128)(2,1)S(1)}, u32[]{:S(2)}, u32[]{:S(2)}) async-start(bf16[8,1,2]{2,1,0:T(2,128)(2,1)} %copy.74), calls=%async_computation.1 | async-start | bytes 8192 | tf_op jit(solution)/shard_map/all_to_all | solution.py:94
  17.7 2.8 gather_fusion
  20.4 4.5 %broadcast_select_fusion.1 = bf16[8,2,128,1024]{3,2,1,0:T(8,128)(2,1)} fusion(bf16[8,2,128,1024]{3,2,1,0:T(8,128)(2,1)} %bitcast.170, pred[8,2]{1,0:T(8,128)(4,1)S(1)} %iota_compare_fusion.4), kind=kLoop, calls=%fused_computation.9 | loop fusion | flops 2097152 | bytes 8388624 | tf_op jit(solution)/shard_map/jit(_where)/select_n | solution.py:88
  24.9 5.2 %all-to-all-start = ((bf16[8,2,128,1024]{3,2,1,0:T(8,128)(2,1)}), bf16[8,2,128,1024]{3,2,1,0:T(8,128)(2,1)}, u32[]{:S(2)}, u32[]{:S(2)}) async-start(bf16[8,2,128,1024]{3,2,1,0:T(8,128)(2,1)} %broadcast_select_fusion.1), calls=%async_computation | async-start | bytes 8388608 | tf_op jit(solution)/shard_map/all_to_all | solution.py:93
  36.6 2.5 all-gather.7.cloned.1.call-done
  39.1 1.9 convolution_convert_fusion.10
  42.3 25.1 %all-gather.11.cloned.1.call-done = bf16[1,512,1024]{2,1,0:T(8,128)(2,1)} async-done(((bf16[1,128,1024]{2,1,0:T(8,128)(2,1)}), bf16[1,512,1024]{2,1,0:T(8,128)(2,1)}) %all-gather.11.cloned.1.call-update) | async-done | bytes 1048592 | tf_op jit(solution)/shard_map/all_gather | solution.py:81
  67.5 1.8 convolution_convert_fusion.9
  70.6 53.6 %all-to-all-done = bf16[8,2,128,1024]{3,2,1,0:T(8,128)(2,1)} async-done(((bf16[8,2,128,1024]{3,2,1,0:T(8,128)(2,1)}), bf16[8,2,128,1024]{3,2,1,0:T(8,128)(2,1)}, u32[]{:S(2)}, u32[]{:S(2)}) %all-to-all-start) | async-done | bytes 4194336 | tf_op jit(solution)/shard_map/all_to_all | solution.py:93
  124.2 4.7 %gather_fusion.2 = bf16[12,128,1024]{2,1,0:T(8,128)(2,1)} fusion(bf16[16,128,1024]{2,1,0:T(8,128)(2,1)} %bitcast.5, s32[1024]{0:T(1024)S(1)} %pad_clamp_fusion.3), kind=kCustom, calls=%fused_computation.2 | custom fusion | bytes 6291504 | tf_op jit(solution)/shard_map/gather | solution.py:108
  129.0 4.0 %convolution_convert_fusion.2 = bf16[12,128,512]{2,1,0:T(8,128)(2,1)S(1)} fusion(bf16[1,1024,512]{2,1,0:T(8,128)(2,1)} %all-gather.9.cloned.1.call-done, bf16[12,128,1024]{2,1,0:T(8,128)(2,1)} %gather_fusion.2, pred[12]{0:T(512)(128)(4,1)S(1)} %iota_compare_fusion.5), kind=kOutput, calls=%fused_computation.30 | convolution fusion | flops 1612972032 | bytes 5767180 | tf_op jit(solution)/shard_map/jvp(ksd,de->kse)/dot_general | solution.py:18
  134.1 4.0 %convolution_convert_fusion.3 = bf16[12,128,512]{2,1,0:T(8,128)(2,1)S(1)} fusion(bf16[1,1024,512]{2,1,0:T(8,128)(2,1)} %all-gather.5.cloned.1.call-done, bf16[12,128,1024]{2,1,0:T(8,128)(2,1)} %gather_fusion.2, pred[12]{0:T(512)(128)(4,1)S(1)} %iota_compare_fusion.5), kind=kOutput, calls=%fused_computation.31 | convolution fusion | flops 1612972032 | bytes 5767180 | tf_op jit(solution)/shard_map/jvp(ksd,de->kse)/dot_general | solution.py:21
  139.7 1.9 select_reduce_fusion
  145.9 1.9 fusion.26
  147.8 3.5 %convert_add_fusion = bf16[12,128,1024]{2,1,0:T(8,128)(2,1)} fusion(bf16[12,128,1024]{2,1,0:T(8,128)(2,1)S(1)} %fusion.26, bf16[12,128,512]{1,2,0:T(8,128)(2,1)S(1)} %bitcast.184, bf16[1,1024,512]{2,1,0:T(8,128)(2,1)S(1)} %copy-done.21), kind=kOutput, calls=%fused_computation.10 | convolution fusion | flops 1613758464 | bytes 8912896 | tf_op jit(solution)/shard_map/transpose(jvp(ksd,de->kse))/dot_general | solution.py:18
  151.3 4.7 %gather_fusion.5 = bf16[16,128,1024]{2,1,0:T(8,128)(2,1)} fusion(bf16[12,128,1024]{2,1,0:T(8,128)(2,1)} %convert_add_fusion, s32[1024]{0:T(1024)S(1)} %pad_clamp_fusion.2), kind=kCustom, calls=%fused_computation.5 | custom fusion | bytes 8388672 | tf_op jit(solution)/shard_map/gather | solution.py:127
  156.0 4.5 %broadcast_select_fusion = bf16[8,2,128,1024]{3,2,1,0:T(8,128)(2,1)} fusion(bf16[8,2,128,1024]{3,2,1,0:T(8,128)(2,1)} %bitcast.169, pred[8,2]{1,0:T(8,128)(4,1)S(1)} %iota_compare_fusion.2), kind=kLoop, calls=%fused_computation.8 | loop fusion | flops 2097152 | bytes 8388624 | tf_op jit(solution)/shard_map/jit(_where)/select_n | solution.py:126
  160.5 4.6 %all-to-all-start.2 = ((bf16[8,2,128,1024]{3,2,1,0:T(8,128)(2,1)}), bf16[8,2,128,1024]{3,2,1,0:T(8,128)(2,1)}, u32[]{:S(2)}, u32[]{:S(2)}) async-start(bf16[8,2,128,1024]{3,2,1,0:T(8,128)(2,1)} %broadcast_select_fusion), calls=%async_computation.2 | async-start | bytes 8388608 | tf_op jit(solution)/shard_map/all_to_all | solution.py:129
  165.1 2.2 fusion.17
  168.5 1.7 reshape.448
  170.2 1.8 fusion.19
  175.0 1.8 bitcast_convert_fusion.3
  177.7 3.1 %bitcast_convert_fusion.2 = bf16[1024,512]{1,0:T(8,128)(2,1)} fusion(bf16[12,128,512]{1,2,0:T(8,128)(2,1)S(1)} %bitcast.185, bf16[12,128,1024]{2,1,0:T(8,128)(2,1)S(1)} %copy-done.6, pred[12]{0:T(512)(128)(4,1)S(1)} %copy-done.28), kind=kOutput, calls=%fused_computation.15 | convolution fusion | flops 1612709888 | bytes 5767180 | tf_op jit(solution)/shard_map/transpose(jvp(ksd,de->kse))/dot_general | solution.py:18
  180.8 3.1 %bitcast_convert_fusion.1 = bf16[1024,512]{1,0:T(8,128)(2,1)} fusion(bf16[12,128,512]{1,2,0:T(8,128)(2,1)S(1)} %bitcast.183, bf16[12,128,1024]{2,1,0:T(8,128)(2,1)S(1)} %copy-done.6, pred[12]{0:T(512)(128)(4,1)S(1)} %copy-done.28), kind=kOutput, calls=%fused_computation.14 | convolution fusion | flops 1612709888 | bytes 5767180 | tf_op jit(solution)/shard_map/transpose(jvp(ksd,de->kse))/dot_general | solution.py:21
  185.3 2.1 fusion.15
  187.4 10.4 %psum.35 = bf16[1024]{0:T(1024)(128)(2,1)S(1)} all-reduce(bf16[1024]{0:T(1024)(128)(2,1)S(1)} %get-tuple-element.8), channel_id=1, replica_groups=mesh['lang'=8,'batch'=4] {'batch'}, use_global_device_ids=true, to_apply=%region_10.11 | all-reduce | flops 1024 | bytes 4096 | tf_op jit(solution)/shard_map/psum | solution.py:141
  198.4 2.7 fusion.18
  202.5 86.7 %all-reduce.3.cloned.1.call-done = (bf16[1024,512]{1,0:T(8,128)(2,1)}, bf16[1024,512]{1,0:T(8,128)(2,1)}, bf16[1024,512]{1,0:T(8,128)(2,1)}, bf16[512,1024]{1,0:T(8,128)(2,1)}) async-done(((bf16[1024,512]{1,0:T(8,128)(2,1)}, bf16[1024,512]{1,0:T(8,128)(2,1)}, bf16[1024,512]{1,0:T(8,128)(2,1)}, bf16[512,1024]{1,0:T(8,128)(2,1)}), (bf16[1024,512]{1,0:T(8,128)(2,1)}, bf16[1024,512]{1,0:T(8,128)(2,1)}, ...) | async-done | bytes 4194320 | tf_op jit(solution)/shard_map/psum | solution.py:137
  289.2 1.8 convert_bitcast_fusion.4
  291.1 1.8 convert_bitcast_fusion.1
  292.8 2.1 convert_bitcast_fusion.2
  295.0 4.1 %gather_fusion.7 = bf16[6,128,1024]{2,1,0:T(8,128)(2,1)} fusion(bf16[16,128,1024]{2,1,0:T(8,128)(2,1)} %bitcast.35, s32[1024]{0:T(1024)S(1)} %pad_clamp_fusion), kind=kCustom, calls=%fused_computation.7 | custom fusion | bytes 3145752 | tf_op jit(solution)/shard_map/gather | solution.py:135
  (128 shorter events, 28.3 us)
Async XLA Ops:
  7.2 10.5 %copy-start = (bf16[1,6,128,1024]{3,2,1,0:T(8,128)(2,1)S(1)}, bf16[1,6,128,1024]{3,2,1,0:T(8,128)(2,1)}, u32[]{:S(2)}) copy-start(bf16[1,6,128,1024]{3,2,1,0:T(8,128)(2,1)} %param.12) | copy-start | bytes 4718596
  7.2 2.5 copy-start.2
  7.2 31.9 %all-gather.7.cloned.1.call-start = ((), (), s32[]{:S(2)}) async-start(), calls=%async_computation.4 | async-start | bytes 1310720 | tf_op jit(solution)/shard_map/all_gather | solution.py:78
  11.2 13.7 %all-to-all-start.1 = ((bf16[8,1,2]{2,1,0:T(2,128)(2,1)}), bf16[8,1,2]{2,1,0:T(2,128)(2,1)S(1)}, u32[]{:S(2)}, u32[]{:S(2)}) async-start(bf16[8,1,2]{2,1,0:T(2,128)(2,1)} %copy.74), calls=%async_computation.1 | async-start | bytes 8192 | tf_op jit(solution)/shard_map/all_to_all | solution.py:94
  24.9 7.3 %copy-start.16 = (s32[8,8]{1,0:T(8,128)S(1)}, s32[8,8]{1,0:T(8,128)}, u32[]{:S(2)}) copy-start(s32[8,8]{1,0:T(8,128)} %param.14) | copy-start | bytes 772
  24.9 99.3 %all-to-all-start = ((bf16[8,2,128,1024]{3,2,1,0:T(8,128)(2,1)}), bf16[8,2,128,1024]{3,2,1,0:T(8,128)(2,1)}, u32[]{:S(2)}, u32[]{:S(2)}) async-start(bf16[8,2,128,1024]{3,2,1,0:T(8,128)(2,1)} %broadcast_select_fusion.1), calls=%async_computation | async-start | bytes 8388608 | tf_op jit(solution)/shard_map/all_to_all | solution.py:93
  30.1 3.9 %copy-start.7 = (bf16[1,12,32,1024]{3,2,1,0:T(8,128)(2,1)S(1)}, bf16[1,12,32,1024]{3,2,1,0:T(8,128)(2,1)}, u32[]{:S(2)}) copy-start(bf16[1,12,32,1024]{3,2,1,0:T(8,128)(2,1)} %param.10) | copy-start | bytes 2359300
  30.2 9.0 %copy-start.17 = (f32[1,1024]{1,0:T(1,128)S(1)}, f32[1,1024]{1,0:T(1,128)}, u32[]{:S(2)}) copy-start(f32[1,1024]{1,0:T(1,128)} %param.15) | copy-start | bytes 12292
  30.2 37.3 %all-gather.11.cloned.1.call-start = ((), (), s32[]{:S(2)}) async-start(), calls=%async_computation.6 | async-start | bytes 1310720 | tf_op jit(solution)/shard_map/all_gather | solution.py:81
  30.9 98.1 %all-gather.9.cloned.1.call-start = ((), (), s32[]{:S(2)}) async-start(), calls=%async_computation.5 | async-start | bytes 1310720 | tf_op jit(solution)/shard_map/all_gather | solution.py:79
  31.6 102.5 %all-gather.5.cloned.1.call-start = ((), (), s32[]{:S(2)}) async-start(), calls=%async_computation.3 | async-start | bytes 1310720 | tf_op jit(solution)/shard_map/all_gather | solution.py:80
  34.4 6.7 %copy-start.14 = (f32[12,32]{1,0:T(8,128)}, f32[12,32]{1,0:T(8,128)S(1)}, u32[]{:S(2)}) copy-start(f32[12,32]{1,0:T(8,128)S(1)} %fusion.41) | copy-start | bytes 4612
  35.0 99.1 %copy-start.27 = (pred[12]{0:T(512)(128)(4,1)}, pred[12]{0:T(512)(128)(4,1)S(1)}, u32[]{:S(2)}) copy-start(pred[12]{0:T(512)(128)(4,1)S(1)} %iota_compare_fusion.5) | copy-start | bytes 40
  39.1 28.4 %copy-start.10 = (bf16[1,12,32,1024]{3,2,1,0:T(8,128)(2,1)S(1)}, bf16[1,12,32,1024]{3,2,1,0:T(8,128)(2,1)}, u32[]{:S(2)}) copy-start(bf16[1,12,32,1024]{3,2,1,0:T(8,128)(2,1)} %param.11) | copy-start | bytes 2359300
  139.7 2.0 copy-start.3
  139.7 2.0 copy-start.9
  141.7 23.4 %copy-start.13 = (f32[12,8,32]{2,1,0:T(8,128)}, f32[12,8,32]{2,1,0:T(8,128)S(1)}, u32[]{:S(2)}) copy-start(f32[12,8,32]{2,1,0:T(8,128)S(1)} %get-tuple-element.19) | copy-start | bytes 36868
  143.9 2.0 copy-start.23
  144.2 1.7 copy-start.22
  145.9 1.9 copy-start.25
  145.9 1.9 copy-start.21
  160.5 134.5 %all-to-all-start.2 = ((bf16[8,2,128,1024]{3,2,1,0:T(8,128)(2,1)}), bf16[8,2,128,1024]{3,2,1,0:T(8,128)(2,1)}, u32[]{:S(2)}, u32[]{:S(2)}) async-start(bf16[8,2,128,1024]{3,2,1,0:T(8,128)(2,1)} %broadcast_select_fusion), calls=%async_computation.2 | async-start | bytes 8388608 | tf_op jit(solution)/shard_map/all_to_all | solution.py:129
  165.0 124.2 %all-reduce.3.cloned.1.call-start = ((), (), s32[]{:S(2)}) async-start(), calls=%async_computation.7 | async-start | bytes 8388608 | tf_op jit(solution)/shard_map/psum | solution.py:137
  167.3 3.0 copy-start.4
  173.2 1.7 copy-start.8
  173.2 1.7 copy-start.15
  173.2 1.7 copy-start.18
  174.9 2.0 copy-start.6
  174.9 2.7 copy-start.26
  174.9 2.7 copy-start.28
  177.7 3.1 %copy-start.24 = (bf16[12,8,64,128]{3,2,1,0:T(8,128)(2,1)S(1)}, bf16[12,8,64,128]{3,2,1,0:T(8,128)(2,1)}, u32[]{:S(2)}) copy-start(bf16[12,8,64,128]{3,2,1,0:T(8,128)(2,1)} %copy-done.23) | copy-start | bytes 4718596
  295.0 4.2 %copy-start.1 = (bf16[1,6,128,1024]{3,2,1,0:T(8,128)(2,1)S(1)}, bf16[1,6,128,1024]{3,2,1,0:T(8,128)(2,1)}, u32[]{:S(2)}) copy-start(bf16[1,6,128,1024]{3,2,1,0:T(8,128)(2,1)} %param.12) | copy-start | bytes 4718596
  (5 other events, 5.1 us)
Sparse Core Ops, SparseCore 0:
  9.8 29.2 all-gather.6
  40.9 26.4 all-gather.10
  69.3 26.4 all-gather.8
  97.5 26.4 all-gather.4
  184.0 105.1 all-reduce.2
where the time goes:
time: 307 us; the launch traced here: 306 us
  waiting for transfers between devices  171 us (56%)
  matrix products  41.3 us (13%)
  local copies, waits for them, and re-layouts  32.6 us (11%)
  other arithmetic  20.1 us (7%)
  starting transfers between devices  16.3 us (5%)
  between operations  14.2 us (5%)
  blocking collectives  10.4 us (3%)
    psum x1, waiting for transfers between devices, per_device(): lax.psum(query_part, 'batch').astype(jnp.float32)  86.7 us
    all_to_all x1, waiting for transfers between devices, per_device(): lax.all_to_all(send_rows, 'lang', split_axis=0, concat_axis=0, tiled=True)  53.6 us
    all_gather x1, waiting for transfers between devices, per_device(): lax.all_gather(w_out, 'batch', axis=1, tiled=True)  25.1 us
    dot_general x3, matrix products, cross_branch(): jnp.einsum('ksd,de->kse', memory, w_key, preferred_element_type=jnp.float32)  10.6 us
    psum x1, blocking collectives, per_device(): lax.psum(gain_part.astype(jnp.bfloat16), 'batch').astype(jnp.float32)  10.4 us
    dot_general x3, matrix products, cross_branch(): jnp.einsum('ksd,de->kse', memory, w_value, preferred_element_type=jnp.flo...  9 us
    all_to_all x1, starting transfers between devices, per_device(): lax.all_to_all(send_lengths, 'lang', split_axis=0, concat_axis=0, tiled=T...  6.35 us
    dot_general x3, matrix products, cross_branch(): jnp.einsum('kte,ed->ktd', context, w_out, preferred_element_type=jnp.floa...  6.26 us
  transfers between devices with their start and end apart: 8, of which 4 were waited for; matrix products, arithmetic and copies ran while one was open for 20% of the time, Pallas kernels for 0%

commit v1 on v0

--- a/solution.py
+++ b/solution.py
@@ -5,6 +5,12 @@
 
 HEADS = 8
 HDIM = 64
+
+
+def summed_here(array, axis):
+    shards = lax.all_gather(array, axis, axis=0, tiled=False)
+    result = shards.sum(axis=0)
+    return result
 
 
 def cross_branch(states, query_gain, w_query, w_key, w_value, w_out, memory, key_lengths):
@@ -134,7 +140,7 @@
     back_index = target_of * pair_cap + sentence_ids - send_start[target_of]
     enc_grad = came_back.reshape(lang_count * pair_cap, seq_len, model_width)[back_index]
     summed = (
-        lax.psum(query_part, "batch").astype(jnp.float32),
+        summed_here(query_part, "batch").astype(jnp.float32),
         lax.psum(key_part, "batch").astype(jnp.float32),
         lax.psum(value_part, "batch").astype(jnp.float32),
         lax.psum(out_part, "batch").astype(jnp.float32),

time: 307 us -> 331 us (1.078)
  waiting for transfers between devices: 171 us -> 183 us
  other arithmetic: 20.1 us -> 27 us
  matrix products: 41.3 us -> 46 us
    all_gather x0 -> x1, waiting for transfers between devices: none -> 51 us  [summed_here(): shards = lax.all_gather(array, axis, axis=0, tiled=False)]
    psum x1, waiting for transfers between devices: 86.7 us -> 37.9 us  [per_device(): lax.psum(key_part, 'batch').astype(jnp.float32)]
    all_to_all x1, waiting for transfers between devices: 53.6 us -> 31.9 us  [per_device(): lax.all_to_all(send_rows, 'lang', split_axis=0, concat_axis=0, tiled=True)]
    all_gather x1, waiting for transfers between devices: 2.54 us -> 23.1 us  [per_device(): lax.all_gather(w_query, 'batch', axis=1, tiled=True)]
    all_gather x1, waiting for transfers between devices: 0.02 us -> 11.8 us  [per_device(): lax.all_gather(w_value, 'batch', axis=1, tiled=True)]
    reduce_sum x0 -> x1, other arithmetic: none -> 3.5 us  [summed_here(): result = shards.sum(axis=0)]
  transfers between devices with their start and end apart: 8 -> 9, of which waited for: 4 -> 6; matrix products, arithmetic and copies ran while one was open for 20% -> 21% of each run, Pallas kernels for 0% -> 0%
where the time goes in v1:
time: 331 us; the launch traced here: 330 us
  waiting for transfers between devices  183 us (55%)
  matrix products  46 us (14%)
  local copies, waits for them, and re-layouts  33 us (10%)
  other arithmetic  27 us (8%)
  starting transfers between devices  16.6 us (5%)
  between operations  14.6 us (4%)
  blocking collectives  9.38 us (3%)
    all_gather x1, waiting for transfers between devices, summed_here(): shards = lax.all_gather(array, axis, axis=0, tiled=False)  51 us
    psum x1, waiting for transfers between devices, per_device(): lax.psum(key_part, 'batch').astype(jnp.float32)  37.9 us
    all_to_all x1, waiting for transfers between devices, per_device(): lax.all_to_all(send_rows, 'lang', split_axis=0, concat_axis=0, tiled=True)  31.9 us
    all_gather x1, waiting for transfers between devices, per_device(): lax.all_gather(w_out, 'batch', axis=1, tiled=True)  25.1 us
    all_gather x1, waiting for transfers between devices, per_device(): lax.all_gather(w_query, 'batch', axis=1, tiled=True)  23.1 us
    all_gather x1, waiting for transfers between devices, per_device(): lax.all_gather(w_value, 'batch', axis=1, tiled=True)  11.8 us
    dot_general x3, matrix products, cross_branch(): jnp.einsum('ksd,de->kse', memory, w_value, preferred_element_type=jnp.flo...  11.4 us
    dot_general x3, matrix products, cross_branch(): jnp.einsum('ksd,de->kse', memory, w_key, preferred_element_type=jnp.float32)  10.6 us
  transfers between devices with their start and end apart: 9, of which 6 were waited for; matrix products, arithmetic and copies ran while one was open for 21% of the time, Pallas kernels for 0%

profile of v1, /device:TPU:0, one launch (start us, length us, event | category | flops | bytes accessed | tf_op | source)
XLA Modules:
  0.0 330.0 jit_solution(13745895144313602420)
XLA Ops:
  10.6 6.4 %all-to-all-start.1 = ((bf16[8,1,2]{2,1,0:T(2,128)(2,1)}), bf16[8,1,2]{2,1,0:T(2,128)(2,1)S(1)}, u32[]{:S(2)}, u32[]{:S(2)}) async-start(bf16[8,1,2]{2,1,0:T(2,128)(2,1)} %copy.74), calls=%async_computation.1 | async-start | bytes 8192 | tf_op jit(solution)/shard_map/all_to_all | solution.py:100
  17.0 2.8 gather_fusion
  19.8 4.5 %broadcast_select_fusion.1 = bf16[8,2,128,1024]{3,2,1,0:T(8,128)(2,1)} fusion(bf16[8,2,128,1024]{3,2,1,0:T(8,128)(2,1)} %bitcast.171, pred[8,2]{1,0:T(8,128)(4,1)S(1)} %iota_compare_fusion.4), kind=kLoop, calls=%fused_computation.9 | loop fusion | flops 2097152 | bytes 8388624 | tf_op jit(solution)/shard_map/jit(_where)/select_n | solution.py:94
  24.3 5.2 %all-to-all-start = ((bf16[8,2,128,1024]{3,2,1,0:T(8,128)(2,1)}), bf16[8,2,128,1024]{3,2,1,0:T(8,128)(2,1)}, u32[]{:S(2)}, u32[]{:S(2)}) async-start(bf16[8,2,128,1024]{3,2,1,0:T(8,128)(2,1)} %broadcast_select_fusion.1), calls=%async_computation | async-start | bytes 8388608 | tf_op jit(solution)/shard_map/all_to_all | solution.py:99
  37.1 23.1 %all-gather.9.cloned.1.call-done = bf16[1,1024,512]{2,1,0:T(8,128)(2,1)} async-done(((bf16[1,256,512]{2,1,0:T(8,128)(2,1)}), bf16[1,1024,512]{2,1,0:T(8,128)(2,1)}) %all-gather.9.cloned.1.call-update) | async-done | bytes 1048592 | tf_op jit(solution)/shard_map/all_gather | solution.py:84
  60.2 1.9 convolution_convert_fusion.10
  63.4 25.1 %all-gather.13.cloned.1.call-done = bf16[1,512,1024]{2,1,0:T(8,128)(2,1)} async-done(((bf16[1,128,1024]{2,1,0:T(8,128)(2,1)}), bf16[1,512,1024]{2,1,0:T(8,128)(2,1)}) %all-gather.13.cloned.1.call-update) | async-done | bytes 1048592 | tf_op jit(solution)/shard_map/all_gather | solution.py:87
  91.7 31.9 %all-to-all-done = bf16[8,2,128,1024]{3,2,1,0:T(8,128)(2,1)} async-done(((bf16[8,2,128,1024]{3,2,1,0:T(8,128)(2,1)}), bf16[8,2,128,1024]{3,2,1,0:T(8,128)(2,1)}, u32[]{:S(2)}, u32[]{:S(2)}) %all-to-all-start) | async-done | bytes 4194336 | tf_op jit(solution)/shard_map/all_to_all | solution.py:99
  123.6 4.8 %gather_fusion.2 = bf16[12,128,1024]{2,1,0:T(8,128)(2,1)} fusion(bf16[16,128,1024]{2,1,0:T(8,128)(2,1)} %bitcast.5, s32[1024]{0:T(1024)S(1)} %pad_clamp_fusion.3), kind=kCustom, calls=%fused_computation.2 | custom fusion | bytes 6291504 | tf_op jit(solution)/shard_map/gather | solution.py:114
  128.4 4.0 %convolution_convert_fusion.2 = bf16[12,128,512]{2,1,0:T(8,128)(2,1)S(1)} fusion(bf16[1,1024,512]{2,1,0:T(8,128)(2,1)} %all-gather.11.cloned.1.call-done, bf16[12,128,1024]{2,1,0:T(8,128)(2,1)} %gather_fusion.2, pred[12]{0:T(512)(128)(4,1)S(1)} %iota_compare_fusion.5), kind=kOutput, calls=%fused_computation.30 | convolution fusion | flops 1612972032 | bytes 5767180 | tf_op jit(solution)/shard_map/jvp(ksd,de->kse)/dot_general | solution.py:24
  133.4 11.8 %all-gather.7.cloned.1.call-done = bf16[1,1024,512]{2,1,0:T(8,128)(2,1)} async-done(((bf16[1,256,512]{2,1,0:T(8,128)(2,1)}), bf16[1,1024,512]{2,1,0:T(8,128)(2,1)}) %all-gather.7.cloned.1.call-update) | async-done | bytes 1048592 | tf_op jit(solution)/shard_map/all_gather | solution.py:86
  145.2 4.0 %convolution_convert_fusion.3 = bf16[12,128,512]{2,1,0:T(8,128)(2,1)S(1)} fusion(bf16[1,1024,512]{2,1,0:T(8,128)(2,1)} %all-gather.7.cloned.1.call-done, bf16[12,128,1024]{2,1,0:T(8,128)(2,1)} %gather_fusion.2, pred[12]{0:T(512)(128)(4,1)S(1)} %iota_compare_fusion.5), kind=kOutput, calls=%fused_computation.31 | convolution fusion | flops 1612972032 | bytes 5767180 | tf_op jit(solution)/shard_map/jvp(ksd,de->kse)/dot_general | solution.py:27
  150.8 1.9 select_reduce_fusion
  153.9 2.3 convolution_convert_fusion.1
  161.2 3.0 bitcast_convert_fusion
  164.2 1.9 convolution_convert_fusion
  166.2 3.1 bitcast_convert_fusion.2
  169.3 3.1 bitcast_convert_fusion.1
  177.6 4.3 %fusion.26 = bf16[12,128,1024]{2,1,0:T(8,128)(2,1)S(1)} fusion(bf16[12,128,512]{1,2,0:T(8,128)(2,1)} %bitcast.184, bf16[1,1024,512]{2,1,0:T(8,128)(2,1)} %all-gather.7.cloned.1.call-done), kind=kOutput, calls=%fused_computation.64 | convolution fusion | flops 1610612736 | bytes 5767168 | tf_op jit(solution)/shard_map/transpose(jvp(ksd,de->kse))/dot_general | solution.py:27
  181.9 3.5 %convert_add_fusion = bf16[12,128,1024]{2,1,0:T(8,128)(2,1)} fusion(bf16[12,128,1024]{2,1,0:T(8,128)(2,1)S(1)} %fusion.26, bf16[12,128,512]{1,2,0:T(8,128)(2,1)S(1)} %bitcast.187, bf16[1,1024,512]{2,1,0:T(8,128)(2,1)S(1)} %copy-done.23), kind=kOutput, calls=%fused_computation.10 | convolution fusion | flops 1613758464 | bytes 8912896 | tf_op jit(solution)/shard_map/transpose(jvp(ksd,de->kse))/dot_general | solution.py:24
  185.4 4.9 %gather_fusion.5 = bf16[16,128,1024]{2,1,0:T(8,128)(2,1)} fusion(bf16[12,128,1024]{2,1,0:T(8,128)(2,1)} %convert_add_fusion, s32[1024]{0:T(1024)} %pad_clamp_fusion.2), kind=kCustom, calls=%fused_computation.5 | custom fusion | bytes 8388672 | tf_op jit(solution)/shard_map/gather | solution.py:133
  190.3 4.5 %broadcast_select_fusion = bf16[8,2,128,1024]{3,2,1,0:T(8,128)(2,1)} fusion(bf16[8,2,128,1024]{3,2,1,0:T(8,128)(2,1)} %bitcast.170, pred[8,2]{1,0:T(8,128)(4,1)} %iota_compare_fusion.2), kind=kLoop, calls=%fused_computation.8 | loop fusion | flops 2097152 | bytes 8388624 | tf_op jit(solution)/shard_map/jit(_where)/select_n | solution.py:132
  194.8 4.8 %all-to-all-start.2 = ((bf16[8,2,128,1024]{3,2,1,0:T(8,128)(2,1)}), bf16[8,2,128,1024]{3,2,1,0:T(8,128)(2,1)}, u32[]{:S(2)}, u32[]{:S(2)}) async-start(bf16[8,2,128,1024]{3,2,1,0:T(8,128)(2,1)} %broadcast_select_fusion), calls=%async_computation.2 | async-start | bytes 8388608 | tf_op jit(solution)/shard_map/all_to_all | solution.py:135
  199.6 2.2 fusion.17
  205.6 2.1 fusion.15
  207.7 9.4 %psum.28 = bf16[1024]{0:T(1024)(128)(2,1)S(1)} all-reduce(bf16[1024]{0:T(1024)(128)(2,1)S(1)} %get-tuple-element.8), channel_id=1, replica_groups=mesh['lang'=8,'batch'=4] {'batch'}, use_global_device_ids=true, to_apply=%region_10.11 | all-reduce | flops 1024 | bytes 4096 | tf_op jit(solution)/shard_map/psum | solution.py:147
  217.7 2.7 fusion.18
  221.9 37.9 %all-reduce.3.cloned.1.call-done = (bf16[1024,512]{1,0:T(8,128)(2,1)}, bf16[1024,512]{1,0:T(8,128)(2,1)}, bf16[512,1024]{1,0:T(8,128)(2,1)}) async-done(((bf16[1024,512]{1,0:T(8,128)(2,1)}, bf16[1024,512]{1,0:T(8,128)(2,1)}, bf16[512,1024]{1,0:T(8,128)(2,1)}), (bf16[1024,512]{1,0:T(8,128)(2,1)}, bf16[1024,512]{1,0:T(8,128)(2,1)}, bf16[512,1024]{1,0:T(8,128)(2,1)})) %all-reduce.3.cloned.1.call-update) | async-done | bytes 3145744 | tf_op jit(solution)/shard_map/psum | solution.py:144
  261.6 2.1 convert_bitcast_fusion.2
  263.7 51.0 %all-gather.15.cloned.1.call-done = bf16[4096,512]{1,0:T(8,128)(2,1)} async-done(((bf16[1024,512]{1,0:T(8,128)(2,1)}), bf16[4096,512]{1,0:T(8,128)(2,1)}) %all-gather.15.cloned.1.call-update) | async-done | bytes 4194320 | tf_op jit(solution)/shard_map/all_gather | solution.py:11
  314.7 3.5 %reduce_sum.107 = bf16[1024,512]{1,0:T(8,128)(2,1)S(1)} reduce(bf16[4,1024,512]{2,1,0:T(8,128)(2,1)} %bitcast.176, bf16[]{:T(256)} %constant.30.clone.1), dimensions={0}, to_apply=%region_11.12 | reduce | flops 1572864 | bytes 5242882 | tf_op jit(solution)/shard_map/reduce_sum | solution.py:12
  319.0 4.1 %gather_fusion.7 = bf16[6,128,1024]{2,1,0:T(8,128)(2,1)} fusion(bf16[16,128,1024]{2,1,0:T(8,128)(2,1)} %bitcast.35, s32[1024]{0:T(1024)S(1)} %pad_clamp_fusion), kind=kCustom, calls=%fused_computation.7 | custom fusion | bytes 3145752 | tf_op jit(solution)/shard_map/gather | solution.py:141
  (132 shorter events, 37.7 us)
Async XLA Ops:
  7.2 9.9 %copy-start = (bf16[1,6,128,1024]{3,2,1,0:T(8,128)(2,1)S(1)}, bf16[1,6,128,1024]{3,2,1,0:T(8,128)(2,1)}, u32[]{:S(2)}) copy-start(bf16[1,6,128,1024]{3,2,1,0:T(8,128)(2,1)} %param.12) | copy-start | bytes 4718596
  7.2 1.9 copy-start.2
  10.6 13.7 %all-to-all-start.1 = ((bf16[8,1,2]{2,1,0:T(2,128)(2,1)}), bf16[8,1,2]{2,1,0:T(2,128)(2,1)S(1)}, u32[]{:S(2)}, u32[]{:S(2)}) async-start(bf16[8,1,2]{2,1,0:T(2,128)(2,1)} %copy.74), calls=%async_computation.1 | async-start | bytes 8192 | tf_op jit(solution)/shard_map/all_to_all | solution.py:100
  24.3 8.1 %copy-start.17 = (s32[8,8]{1,0:T(8,128)S(1)}, s32[8,8]{1,0:T(8,128)}, u32[]{:S(2)}) copy-start(s32[8,8]{1,0:T(8,128)} %param.14) | copy-start | bytes 772
  24.3 99.3 %all-to-all-start = ((bf16[8,2,128,1024]{3,2,1,0:T(8,128)(2,1)}), bf16[8,2,128,1024]{3,2,1,0:T(8,128)(2,1)}, u32[]{:S(2)}, u32[]{:S(2)}) async-start(bf16[8,2,128,1024]{3,2,1,0:T(8,128)(2,1)} %broadcast_select_fusion.1), calls=%async_computation | async-start | bytes 8388608 | tf_op jit(solution)/shard_map/all_to_all | solution.py:99
  29.5 5.1 %copy-start.6 = (bf16[1,12,32,1024]{3,2,1,0:T(8,128)(2,1)S(1)}, bf16[1,12,32,1024]{3,2,1,0:T(8,128)(2,1)}, u32[]{:S(2)}) copy-start(bf16[1,12,32,1024]{3,2,1,0:T(8,128)(2,1)} %param.10) | copy-start | bytes 2359300
  29.5 30.7 %copy-start.18 = (f32[1,1024]{1,0:T(1,128)S(1)}, f32[1,1024]{1,0:T(1,128)}, u32[]{:S(2)}) copy-start(f32[1,1024]{1,0:T(1,128)} %param.15) | copy-start | bytes 12292
  29.5 30.6 %all-gather.9.cloned.1.call-start = ((), (), s32[]{:S(2)}) async-start(), calls=%async_computation.4 | async-start | bytes 1310720 | tf_op jit(solution)/shard_map/all_gather | solution.py:84
  30.3 58.3 %all-gather.13.cloned.1.call-start = ((), (), s32[]{:S(2)}) async-start(), calls=%async_computation.6 | async-start | bytes 1310720 | tf_op jit(solution)/shard_map/all_gather | solution.py:87
  31.0 97.4 %all-gather.11.cloned.1.call-start = ((), (), s32[]{:S(2)}) async-start(), calls=%async_computation.5 | async-start | bytes 1310720 | tf_op jit(solution)/shard_map/all_gather | solution.py:85
  31.8 113.4 %all-gather.7.cloned.1.call-start = ((), (), s32[]{:S(2)}) async-start(), calls=%async_computation.3 | async-start | bytes 1310720 | tf_op jit(solution)/shard_map/all_gather | solution.py:86
  32.3 227.5 %all-reduce.3.cloned.1.call-start = ((), (), s32[]{:S(2)}) async-start(), calls=%async_computation.8 | async-start | bytes 6291456 | tf_op jit(solution)/shard_map/psum | solution.py:144
  34.9 27.2 %copy-start.15 = (f32[12,32]{1,0:T(8,128)}, f32[12,32]{1,0:T(8,128)S(1)}, u32[]{:S(2)}) copy-start(f32[12,32]{1,0:T(8,128)S(1)} %fusion.41) | copy-start | bytes 4612
  35.5 109.6 %copy-start.27 = (pred[12]{0:T(512)(128)(4,1)}, pred[12]{0:T(512)(128)(4,1)S(1)}, u32[]{:S(2)}) copy-start(pred[12]{0:T(512)(128)(4,1)S(1)} %iota_compare_fusion.5) | copy-start | bytes 40
  60.2 28.4 %copy-start.9 = (bf16[1,12,32,1024]{3,2,1,0:T(8,128)(2,1)S(1)}, bf16[1,12,32,1024]{3,2,1,0:T(8,128)(2,1)}, u32[]{:S(2)}) copy-start(bf16[1,12,32,1024]{3,2,1,0:T(8,128)(2,1)} %param.11) | copy-start | bytes 2359300
  150.8 2.0 copy-start.3
  152.8 1.1 copy-start.8
  161.2 3.0 copy-start.4
  161.2 3.0 copy-start.11
  161.2 3.0 copy-start.12
  161.2 3.0 copy-start.14
  164.2 2.0 copy-start.5
  164.2 2.0 copy-start.28
  166.2 3.1 copy-start.25
  166.2 3.1 copy-start.24
  177.6 4.3 %copy-start.23 = (bf16[1,1024,512]{2,1,0:T(8,128)(2,1)S(1)}, bf16[1,1024,512]{2,1,0:T(8,128)(2,1)}, u32[]{:S(2)}) copy-start(bf16[1,1024,512]{2,1,0:T(8,128)(2,1)} %all-gather.11.cloned.1.call-done) | copy-start | bytes 3145732
  177.6 4.3 %copy-start.26 = (bf16[12,8,128,64]{2,3,1,0:T(8,128)(2,1)S(1)}, bf16[12,8,128,64]{2,3,1,0:T(8,128)(2,1)}, u32[]{:S(2)}) copy-start(bf16[12,8,128,64]{2,3,1,0:T(8,128)(2,1)} %copy-done.25) | copy-start | bytes 4718596
  194.8 124.2 %all-to-all-start.2 = ((bf16[8,2,128,1024]{3,2,1,0:T(8,128)(2,1)}), bf16[8,2,128,1024]{3,2,1,0:T(8,128)(2,1)}, u32[]{:S(2)}, u32[]{:S(2)}) async-start(bf16[8,2,128,1024]{3,2,1,0:T(8,128)(2,1)} %broadcast_select_fusion), calls=%async_computation.2 | async-start | bytes 8388608 | tf_op jit(solution)/shard_map/all_to_all | solution.py:135
  199.6 115.1 %all-gather.15.cloned.1.call-start = ((), (), s32[]{:S(2)}) async-start(), calls=%async_computation.7 | async-start | bytes 5242880 | tf_op jit(solution)/shard_map/all_gather | solution.py:11
  203.0 1.9 copy-start.21
  207.7 12.7 %copy-start.10 = (bf16[1,12,32,1024]{3,2,1,0:T(8,128)(2,1)S(1)}, bf16[1,12,32,1024]{3,2,1,0:T(8,128)(2,1)}, u32[]{:S(2)}) copy-start(bf16[1,12,32,1024]{3,2,1,0:T(8,128)(2,1)} %param.11) | copy-start | bytes 2359300
  319.0 4.2 %copy-start.1 = (bf16[1,6,128,1024]{3,2,1,0:T(8,128)(2,1)S(1)}, bf16[1,6,128,1024]{3,2,1,0:T(8,128)(2,1)}, u32[]{:S(2)}) copy-start(bf16[1,6,128,1024]{3,2,1,0:T(8,128)(2,1)} %param.12) | copy-start | bytes 4718596
  (6 other events, 5.7 us)
Sparse Core Ops, SparseCore 0:
  32.2 27.9 all-gather.8
  62.0 26.4 all-gather.12
  90.4 26.4 all-gather.10
  118.6 26.4 all-gather.6
  172.6 87.1 all-reduce.2
  262.1 52.5 all-gather.14
